TPU v7x, 32 devices: a whole 2x2x4 slice. The times are simulated.
32 devices in a mesh: seq: 8 (over z, y), head: 4 (over x, core).
Axes of the slice: x: 2, y: 2, z: 4, core: 2. Of those that a mesh axis runs over, the one named last changes fastest.
Arguments:
- queries: bfloat16 [2048, 2048], P('seq', 'head'), may hold values from -6 to 6
- keys: bfloat16 [2048, 2048], P('seq', 'head'), may hold values from -40 to 40
- values: bfloat16 [2048, 2048], P('seq', 'head'), may hold values from -24 to 24
- ridges: float32 [16], P('head'), may hold values from 0.25 to 4
- out_weight: bfloat16 [2048, 2048], P('head'), may hold values from -0.125 to 0.125
Outputs:
- layer_out: bfloat16 [2048, 2048], P('seq', 'head')
All inputs are finite; a program needn't handle non-finite values.
Results may differ from a plain program's by a relative error of at most 0.0049.
Values may be sent and summed in bfloat16 or wider, within the bound.
A program may use at most 128 MiB of HBM per device.

v0:
```python
import jax
import jax.numpy as jnp
from jax import lax
from jax.sharding import PartitionSpec as P

HD = 128
SPAN = 128
ITERS = 2


highest = lax.Precision.HIGHEST


def carried_in(value, axis, join, neutral):
    count, mine = (lax.axis_size(axis), lax.axis_index(axis))
    pieces = jax.tree.map(lambda part: lax.all_gather(part, axis), value)
    total = jax.tree.map(
        lambda part, zero: jnp.full_like(part, 0) + jnp.asarray(zero, part.dtype), value, neutral
    )

    def step(position, total):
        longer = join(total, jax.tree.map(lambda part: part[position], pieces))
        return jax.tree.map(lambda new, old: jnp.where(position < mine, new, old), longer, total)

    return lax.fori_loop(0, count - 1, step, total)


def normalize(entries):
    return entries * lax.rsqrt(jnp.sum(entries * entries, axis=-1, keepdims=True) + 1e-06)


def split_heads(source, head_count):
    tokens = source.shape[0]
    return source.astype(jnp.float32).reshape(tokens, head_count, -1).transpose(1, 0, 2)


def add_states(earlier, later):
    return (earlier[0] + later[0], earlier[1] + later[1])


def solve_block(queries_b, keyrows, values_b, key_states, value_states, ridges):
    block_len = queries_b.shape[1]
    causal = (
        lax.broadcasted_iota(jnp.int32, (block_len, block_len), 0)
        >= lax.broadcasted_iota(jnp.int32, (block_len, block_len), 1)
    ).astype(jnp.float32)

    def within(inputs, payload):
        scores = jnp.einsum("hck,hsk->hcs", inputs, keyrows, precision=highest) * causal
        return jnp.einsum("hcs,hsk->hck", scores, payload, precision=highest)

    def with_states(inputs, matrices):
        summed = jnp.einsum("hck,hkl->hcl", inputs, matrices[0], precision=highest)
        return summed

    estimate = jnp.zeros_like(queries_b)
    residual = queries_b
    direction = queries_b
    res_norm = jnp.sum(residual * residual, axis=-1, keepdims=True)
    for sweep in range(ITERS):
        applied = (
            ridges[:, None, None] * direction
            + within(direction, keyrows)
            + with_states(direction, key_states)
        )
        step_size = res_norm / (jnp.sum(direction * applied, axis=-1, keepdims=True) + 1e-06)
        estimate = estimate + step_size * direction
        residual = residual - step_size * applied
        fresh = jnp.sum(residual * residual, axis=-1, keepdims=True)
        direction = residual + fresh / (res_norm + 1e-06) * direction
        res_norm = fresh
    return with_states(estimate, value_states) + within(estimate, values_b)


def shards(queries, keys, values, ridges, out_weight):
    head_count = ridges.shape[0]
    tokens = queries.shape[0]
    blocks = tokens // SPAN
    queries_b = normalize(split_heads(queries, head_count)).reshape(head_count, blocks, SPAN, HD)
    keys_b = normalize(split_heads(keys, head_count)).reshape(head_count, blocks, SPAN, HD)
    values_b = split_heads(values, head_count).reshape(head_count, blocks, SPAN, HD)
    key_grams = jnp.einsum("hbck,hbcl->hbkl", keys_b, keys_b, precision=highest)
    value_grams = jnp.einsum("hbck,hbcl->hbkl", keys_b, values_b, precision=highest)
    empty = jnp.zeros((head_count, HD, HD), jnp.float32)
    remote_k, remote_v = carried_in(
        (jnp.sum(key_grams, axis=1), jnp.sum(value_grams, axis=1)),
        "seq",
        add_states,
        (empty, empty),
    )
    local_k = empty
    local_v = empty
    results = []
    for position in range(blocks):
        key_states = (remote_k + local_k,)
        value_states = (remote_v + local_v,)
        results.append(
            solve_block(
                queries_b[:, position],
                keys_b[:, position],
                values_b[:, position],
                key_states,
                value_states,
                ridges,
            )
        )
        local_k = local_k + key_grams[:, position]
        local_v = local_v + value_grams[:, position]
    mixed = (
        jnp.concatenate(results, axis=1)
        .transpose(1, 0, 2)
        .reshape(tokens, head_count * HD)
        .astype(jnp.bfloat16)
    )
    w_columns = lax.all_to_all(out_weight, "head", split_axis=1, concat_axis=0, tiled=True)
    layer_out = jnp.dot(
        lax.all_gather(mixed, "head", axis=1, tiled=True),
        w_columns,
        preferred_element_type=jnp.float32,
    )
    return layer_out.astype(jnp.bfloat16)


def solution(mesh):
    in_specs = (P("seq", "head"), P("seq", "head"), P("seq", "head"), P("head"), P("head", None))
    out_specs = P("seq", "head")
    return jax.shard_map(shards, mesh=mesh, in_specs=in_specs, out_specs=out_specs, check_vma=False)
```

profile of v0, /device:TPU:25, one launch (start us, length us, event | category | flops | bytes accessed | tf_op | source)
XLA Modules:
  0.0 152.4 jit_solution(17580866851601486464)
XLA Ops:
  6.5 0.0 all-gather.8.cloned.1.call-start
  6.5 1.1 copy.75
  7.6 0.0 copy-start.2
  7.6 0.1 fusion.8
  7.8 0.2 copy.76
  8.0 0.0 copy-start
  8.0 1.7 %fusion.20 = (f32[4,128,128]{2,1,0:T(8,128)}, f32[4,2,128,128]{3,2,1,0:T(8,128)S(1)}) fusion(f32[4,2,128,128]{3,2,1,0:T(8,128)S(1)} %bitcast.146), kind=kOutput, calls=%fused_computation.68 | convolution fusion | flops 201392128 | bytes 1310720 | tf_op jit(solution)/shard_map/hbck,hbcl->hbkl/dot_general | solution.py:82
  9.7 0.0 all-gather.8.cloned.1.call-update
  9.7 0.0 all-gather.10.cloned.1.call-start
  9.8 0.0 copy-done.2
  9.8 0.8 copy.81
  10.6 1.1 copy.82
  11.7 2.2 %fusion.21 = (f32[4,128,128]{2,1,0:T(8,128)}, f32[4,2,128,128]{3,2,1,0:T(8,128)}) fusion(f32[4,2,128,128]{3,2,1,0:T(8,128)S(1)} %bitcast.147, bf16[4,2,128,128]{3,2,1,0:T(8,128)(2,1)S(1)} %bitcast.172), kind=kOutput, calls=%fused_computation.69 | convolution fusion | flops 201392128 | bytes 1572864 | tf_op jit(solution)/shard_map/hbck,hbcl->hbkl/dot_general | solution.py:83
  13.9 0.0 all-gather.10.cloned.1.call-update
  13.9 0.0 copy-done
  14.0 2.6 %copy.103 = bf16[512,2048]{0,1:T(8,128)(2,1)} copy(bf16[512,2048]{1,0:T(8,128)(2,1)S(1)} %copy-done) | data formatting | bytes 4194304 | tf_op args[4]
  16.5 0.0 copy-start.3
  16.5 5.2 %all-to-all-start = ((bf16[512,4,512]{0,2,1:T(8,128)(2,1)}), bf16[512,4,512]{0,2,1:T(8,128)(2,1)}, u32[]{:S(2)}, u32[]{:S(2)}) async-start(bf16[512,4,512]{0,2,1:T(8,128)(2,1)} %bitcast.23), calls=%async_computation | async-start | bytes 4194304 | tf_op jit(solution)/shard_map/all_to_all | solution.py:115
  21.7 0.0 all-gather.6.cloned.1.call-start
  21.7 0.0 copy-done.3
  21.7 0.0 copy-start.4
  21.8 0.1 copy.72
  21.9 0.1 fusion.11
  22.0 0.2 copy.73
  22.3 0.7 convolution_multiply_fusion.5
  22.9 0.7 convolution_multiply_fusion.2
  23.6 0.0 copy-done.4
  23.6 0.4 convolution_add_fusion.9
  24.0 0.4 convolution_add_fusion.4
  24.4 33.5 %all-gather.8.cloned.1.call-done = f32[32,128,128]{2,1,0:T(8,128)} async-done(((f32[4,128,128]{2,1,0:T(8,128)}), f32[32,128,128]{2,1,0:T(8,128)}) %all-gather.8.cloned.1.call-update) | async-done | bytes 2097168 | tf_op jit(solution)/shard_map/all_gather | solution.py:16
  57.9 49.8 %all-gather.10.cloned.1.call-done = f32[32,128,128]{2,1,0:T(8,128)} async-done(((f32[4,128,128]{2,1,0:T(8,128)}), f32[32,128,128]{2,1,0:T(8,128)}) %all-gather.10.cloned.1.call-update) | async-done | bytes 2097168 | tf_op jit(solution)/shard_map/all_gather | solution.py:16
  107.7 8.7 %while.16 = (s32[]{:T(128)}, f32[4,128,128]{2,1,0:T(8,128)S(1)}, f32[4,128,128]{2,1,0:T(8,128)S(1)}, s32[]{:T(128)}, f32[8,4,128,128]{3,2,1,0:T(8,128)}, /*index=5*/f32[8,4,128,128]{3,2,1,0:T(8,128)}, s32[]{:T(128)}, s32[]{:T(128)}) while((s32[]{:T(128)}, f32[4,128,128]{2,1,0:T(8,128)S(1)}, f32[4,128,128]{2,1,0:T(8,128)S(1)}, ...), condition=%wide.region_6.7_spmd.clone, body=%wide.region_5.6_spmd.clone.sunk | while | flops 393220 | bytes 1572981 | solution.py:25
  107.7 1.2 add_select_fusion.3
  108.9 1.2 add_select_fusion.3
  110.2 1.2 add_select_fusion.3
  111.4 1.2 add_select_fusion.3
  112.7 1.2 add_select_fusion.3
  113.9 1.2 add_select_fusion.3
  115.2 1.2 add_select_fusion.3
  116.4 0.5 multiply_reduce_fusion.4
  117.0 0.6 multiply_reduce_fusion.3
  117.5 0.4 multiply_add_fusion.3
  117.9 0.7 convolution_multiply_fusion.4
  118.6 0.4 convolution_add_fusion.7
  119.0 0.5 fusion.4
  119.5 0.2 multiply_add_fusion.1
  119.7 0.7 convolution_multiply_fusion.1
  120.4 0.4 convolution_add_fusion.2
  120.8 0.0 copy-start.1
  120.8 0.5 fusion.5
  121.4 0.8 convolution_multiply_fusion
  122.1 0.8 convolution_multiply_fusion.3
  122.9 0.5 fusion.18
  123.4 0.0 copy-done.1
  123.4 0.5 fusion.13
  124.0 0.3 fusion.3
  124.2 0.3 fusion.2
  124.5 0.9 copy.102
  125.4 0.0 all-gather.6.cloned.1.call-update
  125.4 0.0 all-to-all-done
  125.4 2.8 %copy.104 = bf16[4,512,512]{2,1,0:T(8,128)(2,1)S(1)} copy(bf16[4,512,512]{1,2,0:T(8,128)(2,1)} %bitcast.24) | data formatting | bytes 4194304 | tf_op jit(solution)/shard_map/all_to_all | solution.py:115
  128.2 15.0 %all-gather.6.cloned.1.call-done = bf16[256,2048]{0,1:T(8,128)(2,1)} async-done(((bf16[256,512]{0,1:T(8,128)(2,1)}), bf16[256,2048]{0,1:T(8,128)(2,1)}) %all-gather.6.cloned.1.call-update) | async-done | bytes 1048592 | tf_op jit(solution)/shard_map/all_gather | solution.py:117
  143.2 2.7 %convolution_convert_fusion = bf16[256,512]{1,0:T(8,128)(2,1)} fusion(bf16[256,2048]{0,1:T(8,128)(2,1)} %all-gather.6.cloned.1.call-done, bf16[2048,512]{1,0:T(8,128)(2,1)S(1)} %bitcast.175), kind=kOutput, calls=%fused_computation.2 | convolution fusion | flops 537001984 | bytes 3407872 | tf_op jit(solution)/shard_map/dot_general | solution.py:116
  (13 shorter events, 0.2 us)
Async XLA Ops:
  6.5 51.4 %all-gather.8.cloned.1.call-start = ((), (), s32[]{:S(2)}) async-start(), calls=%async_computation.2 | async-start | bytes 2359296 | tf_op jit(solution)/shard_map/all_gather | solution.py:16
  7.6 2.2 %copy-start.2 = (bf16[256,512]{1,0:T(8,128)(2,1)S(1)}, bf16[256,512]{1,0:T(8,128)(2,1)}, u32[]{:S(2)}) copy-start(bf16[256,512]{1,0:T(8,128)(2,1)} %param.9) | copy-start | bytes 786436
  8.0 6.0 %copy-start = (bf16[512,2048]{1,0:T(8,128)(2,1)S(1)}, bf16[512,2048]{1,0:T(8,128)(2,1)}, u32[]{:S(2)}) copy-start(bf16[512,2048]{1,0:T(8,128)(2,1)} %param.11) | copy-start | bytes 6291460
  9.7 97.9 %all-gather.10.cloned.1.call-start = ((), (), s32[]{:S(2)}) async-start(), calls=%async_computation.3 | async-start | bytes 2359296 | tf_op jit(solution)/shard_map/all_gather | solution.py:16
  16.5 5.2 %copy-start.3 = (bf16[256,512]{1,0:T(8,128)(2,1)S(1)}, bf16[256,512]{1,0:T(8,128)(2,1)}, u32[]{:S(2)}) copy-start(bf16[256,512]{1,0:T(8,128)(2,1)} %param.7) | copy-start | bytes 786436
  16.5 108.9 %all-to-all-start = ((bf16[512,4,512]{0,2,1:T(8,128)(2,1)}), bf16[512,4,512]{0,2,1:T(8,128)(2,1)}, u32[]{:S(2)}, u32[]{:S(2)}) async-start(bf16[512,4,512]{0,2,1:T(8,128)(2,1)} %bitcast.23), calls=%async_computation | async-start | bytes 4194304 | tf_op jit(solution)/shard_map/all_to_all | solution.py:115
  21.7 121.5 %all-gather.6.cloned.1.call-start = ((), (), s32[]{:S(2)}) async-start(), calls=%async_computation.1 | async-start | bytes 1310720 | tf_op jit(solution)/shard_map/all_gather | solution.py:117
  21.7 1.8 %copy-start.4 = (f32[4]{0:T(128)S(1)}, f32[4]{0:T(128)}, u32[]{:S(2)}) copy-start(f32[4]{0:T(128)} %param.10) | copy-start | bytes 52
  120.8 2.6 %copy-start.1 = (f32[4,2,128,128]{3,2,1,0:T(8,128)S(1)}, f32[4,2,128,128]{3,2,1,0:T(8,128)}, u32[]{:S(2)}) copy-start(f32[4,2,128,128]{3,2,1,0:T(8,128)} %get-tuple-element.162) | copy-start | bytes 1572868
Sparse Core Ops, SparseCore 0:
  9.8 48.0 all-gather.7
  60.0 47.6 all-gather.9
  125.5 17.6 all-gather.5
where the time goes:
time: 154 us; the launch traced here: 152 us
  waiting for transfers between devices  98.3 us (64%)
  matrix products  16 us (10%)
  between operations  13.4 us (9%)
  local copies, waits for them, and re-layouts  9.76 us (6%)
  other arithmetic  9.46 us (6%)
  starting transfers between devices  5.27 us (3%)
    all_gather x2, waiting for transfers between devices, carried_in(): pieces = jax.tree.map(lambda part: lax.all_gather(part, axis), value)  83.3 us
    all_gather x1, waiting for transfers between devices, shards(): lax.all_gather(mixed, 'head', axis=1, tiled=True)  15 us
    select_n x7, other arithmetic, step(): jnp.where(position < mine, new, old)  8.58 us
    all_to_all x1, starting transfers between devices, shards(): lax.all_to_all(out_weight, 'head', split_axis=1, concat_axis=0, tiled=True)  5.23 us
    unnamed x14, local copies, waits for them, and re-layouts  4.63 us
    dot_general x6, matrix products, within(): jnp.einsum('hck,hsk->hcs', inputs, keyrows, precision=highest) * causal  4.21 us
    dot_general x6, matrix products, with_states(): summed = jnp.einsum('hck,hkl->hcl', inputs, matrices[0], precision=highest)  3.17 us
  transfers between devices with their start and end apart: 4, of which 3 were waited for; matrix products, arithmetic and copies ran while one was open for 19% of the time, Pallas kernels for 0%

commit v1 on v0

v1 whole, which is shorter than its diff:
```python
import functools

import jax
import jax.numpy as jnp
from jax import lax
from jax.experimental import pallas as pl
from jax.experimental.pallas import tpu as pltpu
from jax.sharding import PartitionSpec as P

MESH = pl.DeviceIdType.MESH
EPS = 1e-06


def split(value):
    high = value.astype(jnp.bfloat16)
    return high, (value - high.astype(jnp.float32)).astype(jnp.bfloat16)


def product(left, right, dims=((1,), (0,))):
    return lax.dot_general(left, right, (dims, ((), ())), preferred_element_type=jnp.float32)


def row_sum(value):
    return jnp.sum(value, axis=-1, keepdims=True)


def kernel(
    seqs, groups, heads,
    q_any, k_any, v_any, ridge_ref, w_any, out_ref,
    q_ref, k_ref, v_ref, w_own, w_other,
    high_ref, low_ref, sums, sums_out, sums_in, run_out, run_in,
    qn_ref, first, mixed, mixed_in, part_out, part_in,
    load_sem, w_sem, ws_sem, wr_sem, ss_sem, sr_sem, rs_sem, rr_sem, ms_sem, mr_sem, ps_sem, pr_sem,
):
    seq, group = lax.axis_index("seq"), lax.axis_index("head")
    rank, side = seq // 2, seq % 2
    pair, lane = group // 2, group % 2
    ranks, pairs = seqs // 2, groups // 2
    tokens, width = out_ref.shape
    hd = q_ref.shape[1] // heads
    twin_seq, twin_head = seq + 1 - 2 * side, group + 1 - 2 * lane
    not_first, not_last = rank > 0, rank < ranks - 1

    loads = [
        pltpu.make_async_copy(src, dst, load_sem.at[at])
        for at, (src, dst) in enumerate(((k_any, k_ref), (v_any, v_ref), (q_any, q_ref)))
    ]
    for load in loads:
        load.start()

    def columns(at, parity):
        return pl.ds(pl.multiple_of((2 * at + parity) * width, 128), width)

    w_loads = [
        pltpu.make_async_copy(w_any.at[:, columns(at, lane)], w_own.at[at], w_sem.at[at])
        for at in range(pairs)
    ]
    for load in w_loads:
        load.start()

    barrier = pltpu.get_barrier_semaphore()

    def greet(**device):
        pl.semaphore_signal(barrier, inc=1, device_id=device, device_id_type=MESH)

    greet(seq=twin_seq)
    greet(head=twin_head)
    for off in range(1, pairs):
        greet(head=2 * ((pair + off) % pairs) + lane)

    @pl.when(not_first)
    def _():
        greet(seq=seq - 2)

    @pl.when(not_last)
    def _():
        greet(seq=seq + 2)

    pl.semaphore_wait(
        barrier, pairs + 1 + not_first.astype(jnp.int32) + not_last.astype(jnp.int32)
    )

    w_sends = [
        pltpu.make_async_remote_copy(
            w_any.at[:, columns(at, 1 - lane)], w_other.at[at], ws_sem.at[at], wr_sem.at[at],
            device_id={"head": twin_head}, device_id_type=MESH,
        )
        for at in range(pairs)
    ]

    loads[0].wait()
    loads[1].wait()
    sum_sends = []
    for at in range(heads):
        span = slice(at * hd, (at + 1) * hd)
        keys = k_ref[:, span].astype(jnp.float32)
        scale = lax.rsqrt(row_sum(keys * keys) + EPS)
        payload = jnp.concatenate(
            [keys * (scale * scale), v_ref[:, span].astype(jnp.float32) * scale], axis=1
        )
        high, low = split(payload)
        high_ref[at] = high
        low_ref[at] = low
        both = ((0,), (0,))
        total = product(k_ref[:, span], high, both) + product(k_ref[:, span], low, both)
        sums[at] = total
        sums_out[at] = total.astype(jnp.bfloat16)
        send = pltpu.make_async_remote_copy(
            sums_out.at[at], sums_in.at[at], ss_sem.at[at], sr_sem.at[at],
            device_id={"seq": twin_seq}, device_id_type=MESH,
        )
        send.start()
        sum_sends.append(send)

    for send in w_sends:
        send.start()

    causal = lax.broadcasted_iota(jnp.int32, (tokens, tokens), 0) >= lax.broadcasted_iota(
        jnp.int32, (tokens, tokens), 1
    )

    def within(at, parts):
        keys = k_ref[:, at * hd:(at + 1) * hd]
        across = ((1,), (1,))
        scores = product(parts[0], keys, across) + product(parts[1], keys, across)
        high, low = split(jnp.where(causal, scores, 0.0))
        payload = high_ref[at]
        return product(high, payload) + product(low, payload) + product(high, low_ref[at])

    loads[2].wait()
    for at in range(heads):
        q = q_ref[:, at * hd:(at + 1) * hd].astype(jnp.float32)
        q = q * lax.rsqrt(row_sum(q * q) + EPS)
        qn_ref[at] = q
        first[at] = within(at, split(q))

    mixed_sends = []
    run_sends = []
    for at in range(heads):
        run_sends.append(pltpu.make_async_remote_copy(
            run_out.at[at], run_in.at[at], rs_sem.at[at], rr_sem.at[at],
            device_id={"seq": (seq + 2) % seqs}, device_id_type=MESH,
        ))

        @pl.when(rank == 0)
        def _():
            run_in[at] = jnp.zeros(run_in.shape[1:], run_in.dtype)

        sum_sends[at].wait_recv()

        @pl.when(not_first)
        def _():
            run_sends[at].wait_recv()

        @pl.when(not_last)
        def _():
            run_out[at] = (
                run_in[at].astype(jnp.float32) + (sums[at] + sums_in[at].astype(jnp.float32))
            ).astype(jnp.bfloat16)
            run_sends[at].start()

        near = jnp.where(side == 1, sums_in[at], jnp.zeros(sums_in.shape[1:], jnp.bfloat16))
        state = jnp.concatenate([run_in[at], near], axis=0)

        def carried(parts):
            high, low = parts
            return product(jnp.concatenate([high, high], axis=1), state) + product(
                jnp.concatenate([low, low], axis=1), state
            )

        ridge = ridge_ref[at]
        q = qn_ref[at]
        whole = first[at] + carried(split(q))
        norm = row_sum(q * q)
        applied = whole[:, :hd] + ridge * q
        step = norm / (row_sum(q * applied) + EPS)
        residual = q - step * applied
        fresh = row_sum(residual * residual)
        direction = residual + fresh / (norm + EPS) * q
        parts = split(direction)
        again = within(at, parts) + carried(parts)
        applied = again[:, :hd] + ridge * direction
        after = fresh / (row_sum(direction * applied) + EPS)
        span = slice(at * hd, (at + 1) * hd)
        mixed[:, span] = (step * whole[:, hd:] + after * again[:, hd:]).astype(jnp.bfloat16)
        send = pltpu.make_async_remote_copy(
            mixed.at[:, span], mixed_in.at[:, span], ms_sem.at[at], mr_sem.at[at],
            device_id={"head": twin_head}, device_id_type=MESH,
        )
        send.start()
        mixed_sends.append(send)

    for load in w_loads:
        load.wait()
    for send in w_sends:
        send.wait_recv()
    for send in mixed_sends:
        send.wait_recv()

    def projected(index, rows):
        return product(mixed[rows, :], w_own[index]) + product(mixed_in[rows, :], w_other[index])

    cuts = part_out.shape[1]
    cut = tokens // cuts
    part_sends = []
    for off in range(1, pairs):
        target = (pair + off) % pairs
        for piece in range(cuts):
            part_out[off - 1, piece] = projected(
                target, slice(piece * cut, (piece + 1) * cut)
            ).astype(jnp.bfloat16)
            send = pltpu.make_async_remote_copy(
                part_out.at[off - 1, piece], part_in.at[off - 1, piece],
                ps_sem.at[off - 1, piece], pr_sem.at[off - 1, piece],
                device_id={"head": 2 * target + lane}, device_id_type=MESH,
            )
            send.start()
            part_sends.append(send)
    own = [projected(pair, slice(piece * cut, (piece + 1) * cut)) for piece in range(cuts)]
    for piece in range(cuts):
        total = own[piece]
        for off in range(1, pairs):
            part_sends[(off - 1) * cuts + piece].wait_recv()
            total = total + part_in[off - 1, piece].astype(jnp.float32)
        out_ref[piece * cut:(piece + 1) * cut, :] = total.astype(out_ref.dtype)

    for send in sum_sends + w_sends + mixed_sends + part_sends:
        send.wait_send()

    @pl.when(not_last)
    def _():
        for send in run_sends:
            send.wait_send()


def solution(mesh):
    seqs, groups = mesh.shape["seq"], mesh.shape["head"]

    def shards(queries, keys, values, ridges, out_weight):
        tokens, wide = queries.shape
        heads = ridges.shape[0]
        hd = wide // heads
        rows, model = out_weight.shape
        width = model // groups
        pairs = groups // 2
        cuts = 4
        bf16, f32 = jnp.bfloat16, jnp.float32
        dma = pltpu.SemaphoreType.DMA
        others = max(pairs - 1, 1)
        any_spec = pl.BlockSpec(memory_space=pl.ANY)
        return pl.pallas_call(
            functools.partial(kernel, seqs, groups, heads),
            out_shape=jax.ShapeDtypeStruct((tokens, width), bf16),
            in_specs=[any_spec, any_spec, any_spec, pl.BlockSpec(memory_space=pltpu.SMEM), any_spec],
            out_specs=pl.BlockSpec(memory_space=pltpu.VMEM),
            scratch_shapes=[
                pltpu.VMEM((tokens, wide), bf16),
                pltpu.VMEM((tokens, wide), bf16),
                pltpu.VMEM((tokens, wide), bf16),
                pltpu.VMEM((pairs, rows, width), bf16),
                pltpu.VMEM((pairs, rows, width), bf16),
                pltpu.VMEM((heads, tokens, 2 * hd), bf16),
                pltpu.VMEM((heads, tokens, 2 * hd), bf16),
                pltpu.VMEM((heads, hd, 2 * hd), f32),
                pltpu.VMEM((heads, hd, 2 * hd), bf16),
                pltpu.VMEM((heads, hd, 2 * hd), bf16),
                pltpu.VMEM((heads, hd, 2 * hd), bf16),
                pltpu.VMEM((heads, hd, 2 * hd), bf16),
                pltpu.VMEM((heads, tokens, hd), f32),
                pltpu.VMEM((heads, tokens, 2 * hd), f32),
                pltpu.VMEM((tokens, wide), bf16),
                pltpu.VMEM((tokens, wide), bf16),
                pltpu.VMEM((others, cuts, tokens // cuts, width), bf16),
                pltpu.VMEM((others, cuts, tokens // cuts, width), bf16),
                dma((3,)), dma((pairs,)), dma((pairs,)), dma((pairs,)),
                dma((heads,)), dma((heads,)), dma((heads,)), dma((heads,)),
                dma((heads,)), dma((heads,)), dma((others, cuts)), dma((others, cuts)),
            ],
            compiler_params=pltpu.CompilerParams(
                collective_id=0, has_side_effects=True, vmem_limit_bytes=48 * 2**20
            ),
        )(queries, keys, values, ridges, out_weight)

    in_specs = (P("seq", "head"), P("seq", "head"), P("seq", "head"), P("head"), P("head", None))
    return jax.shard_map(
        shards, mesh=mesh, in_specs=in_specs, out_specs=P("seq", "head"), check_vma=False
    )
```

time: 154 us -> 36.7 us (0.24)
  waiting for transfers between devices: 98.3 us -> 0 us
  Pallas kernels: 0 us -> 30.6 us
  matrix products: 16 us -> 0 us
  between operations: 13.4 us -> 0.01 us
  other arithmetic: 9.46 us -> 0 us
  starting transfers between devices: 5.27 us -> 0 us
  local copies, waits for them, and re-layouts: 9.76 us -> 5.8 us
    all_gather x3 -> x0, waiting for transfers between devices: 98.3 us -> none  [the longest x2 83.3 us: carried_in(): pieces = jax.tree.map(lambda part: lax.all_gather(part, axis), value)]
    pallas_call x0 -> x1, Pallas kernels: none -> 30.6 us  [shards(): pl.pallas_call(functools.partial(kernel, seqs, groups, heads), out_shape=...]
    dot_general x21 -> x0, matrix products: 16 us -> none  [the longest x6 4.21 us: within(): jnp.einsum('hck,hsk->hcs', inputs, keyrows, precision=highest) * causal]
    select_n x7 -> x0, other arithmetic: 8.58 us -> none  [step(): jnp.where(position < mine, new, old)]
    all_to_all x1 -> x0, starting transfers between devices: 5.23 us -> none  [shards(): lax.all_to_all(out_weight, 'head', split_axis=1, concat_axis=0, tiled=True)]
    all_to_all x1 -> x0, local copies, waits for them, and re-layouts: 2.79 us -> none  [shards(): lax.all_to_all(out_weight, 'head', split_axis=1, concat_axis=0, tiled=True)]
    unnamed x14 -> x11, local copies, waits for them, and re-layouts: 4.63 us -> 5.8 us
  transfers between devices with their start and end apart: 4 -> 0, of which waited for: 3 -> 0; matrix products, arithmetic and copies ran while one was open for 19% -> 0% of each run, Pallas kernels for 0% -> 0%
where the time goes in v1:
time: 36.7 us; the launch traced here: 36.4 us
  Pallas kernels  30.6 us (83%)
  local copies, waits for them, and re-layouts  5.8 us (16%)
    pallas_call x1, Pallas kernels, shards(): pl.pallas_call(functools.partial(kernel, seqs, groups, heads), out_shape=...  30.6 us
    unnamed x11, local copies, waits for them, and re-layouts  5.8 us

profile of v1, /device:TPU:25, one launch (start us, length us, event | category | flops | bytes accessed | tf_op | source)
XLA Modules:
  0.0 36.4 jit_solution(9181972700228493490)
XLA Ops:
  0.0 0.0 copy-start
  0.0 1.6 %copy-done = bf16[512,2048]{1,0:T(8,128)(2,1)S(1)} copy-done((bf16[512,2048]{1,0:T(8,128)(2,1)S(1)}, bf16[512,2048]{1,0:T(8,128)(2,1)}, u32[]{:S(2)}) %copy-start) | copy-done | bytes 2097176
  1.6 0.0 copy-start.1
  1.6 0.9 %copy-done.1 = bf16[256,512]{1,0:T(8,128)(2,1)S(1)} copy-done((bf16[256,512]{1,0:T(8,128)(2,1)S(1)}, bf16[256,512]{1,0:T(8,128)(2,1)}, u32[]{:S(2)}) %copy-start.1) | copy-done | bytes 262168
  2.5 0.0 copy-start.2
  2.5 0.9 %copy-done.2 = bf16[256,512]{1,0:T(8,128)(2,1)S(1)} copy-done((bf16[256,512]{1,0:T(8,128)(2,1)S(1)}, bf16[256,512]{1,0:T(8,128)(2,1)}, u32[]{:S(2)}) %copy-start.2) | copy-done | bytes 262168
  3.5 0.0 copy-start.3
  3.5 0.9 %copy-done.3 = bf16[256,512]{1,0:T(8,128)(2,1)S(1)} copy-done((bf16[256,512]{1,0:T(8,128)(2,1)S(1)}, bf16[256,512]{1,0:T(8,128)(2,1)}, u32[]{:S(2)}) %copy-start.3) | copy-done | bytes 262168
  4.4 0.0 copy-start.4
  4.4 0.7 %copy-done.4 = f32[4]{0:T(128)S(1)} copy-done((f32[4]{0:T(128)S(1)}, f32[4]{0:T(128)}, u32[]{:S(2)}) %copy-start.4) | copy-done | bytes 40
  5.1 30.6 %shard_map.55 = bf16[256,512]{1,0:T(8,128)(2,1)S(1)} custom-call(bf16[256,512]{1,0:T(8,128)(2,1)S(1)} %copy-done.1, bf16[256,512]{1,0:T(8,128)(2,1)S(1)} %copy-done.2, bf16[256,512]{1,0:T(8,128)(2,1)S(1)} %copy-done.3, f32[4]{0:T(128)S(1)} %copy-done.4, bf16[512,2048]{1,0:T(8,128)(2,1)S(1)} %copy-done), custom_call_target="tpu_custom_call" | custom-call | tf_op jit(solution)/shard_map/pallas_call | solution.py:251
  35.7 0.7 %copy.7 = bf16[256,512]{1,0:T(8,128)(2,1)} copy(bf16[256,512]{1,0:T(8,128)(2,1)S(1)} %shard_map.55) | data formatting | bytes 524288
Async XLA Ops:
  0.0 1.6 %copy-start = (bf16[512,2048]{1,0:T(8,128)(2,1)S(1)}, bf16[512,2048]{1,0:T(8,128)(2,1)}, u32[]{:S(2)}) copy-start(bf16[512,2048]{1,0:T(8,128)(2,1)} %w_any.1) | copy-start | bytes 6291460
  1.6 0.9 %copy-start.1 = (bf16[256,512]{1,0:T(8,128)(2,1)S(1)}, bf16[256,512]{1,0:T(8,128)(2,1)}, u32[]{:S(2)}) copy-start(bf16[256,512]{1,0:T(8,128)(2,1)} %q_any.1) | copy-start | bytes 786436
  2.5 0.9 %copy-start.2 = (bf16[256,512]{1,0:T(8,128)(2,1)S(1)}, bf16[256,512]{1,0:T(8,128)(2,1)}, u32[]{:S(2)}) copy-start(bf16[256,512]{1,0:T(8,128)(2,1)} %k_any.1) | copy-start | bytes 786436
  3.5 0.9 %copy-start.3 = (bf16[256,512]{1,0:T(8,128)(2,1)S(1)}, bf16[256,512]{1,0:T(8,128)(2,1)}, u32[]{:S(2)}) copy-start(bf16[256,512]{1,0:T(8,128)(2,1)} %v_any.1) | copy-start | bytes 786436
  4.4 0.7 %copy-start.4 = (f32[4]{0:T(128)S(1)}, f32[4]{0:T(128)}, u32[]{:S(2)}) copy-start(f32[4]{0:T(128)} %ridge_ref.1) | copy-start | bytes 52

commit v2 on v1

--- a/solution.py
+++ b/solution.py
@@ -28,9 +28,9 @@
     seqs, groups, heads,
     q_any, k_any, v_any, ridge_ref, w_any, out_ref,
     q_ref, k_ref, v_ref, w_own, w_other,
-    high_ref, low_ref, sums, sums_out, sums_in, run_out, run_in,
+    high_ref, low_ref, sums, sums_out, sums_in, run_out, run_in, past_out, past_in,
     qn_ref, first, mixed, mixed_in, part_out, part_in,
-    load_sem, w_sem, ws_sem, wr_sem, ss_sem, sr_sem, rs_sem, rr_sem, ms_sem, mr_sem, ps_sem, pr_sem,
+    load_sem, w_sem, ws_sem, wr_sem, ss_sem, sr_sem, rs_sem, rr_sem, as_sem, ar_sem, ms_sem, mr_sem, ps_sem, pr_sem,
 ):
     seq, group = lax.axis_index("seq"), lax.axis_index("head")
     rank, side = seq // 2, seq % 2
@@ -76,10 +76,6 @@
     def _():
         greet(seq=seq + 2)
 
-    pl.semaphore_wait(
-        barrier, pairs + 1 + not_first.astype(jnp.int32) + not_last.astype(jnp.int32)
-    )
-
     w_sends = [
         pltpu.make_async_remote_copy(
             w_any.at[:, columns(at, 1 - lane)], w_other.at[at], ws_sem.at[at], wr_sem.at[at],
@@ -90,6 +86,7 @@
 
     loads[0].wait()
     loads[1].wait()
+    near, far = side, 1 - side
     sum_sends = []
     for at in range(heads):
         span = slice(at * hd, (at + 1) * hd)
@@ -103,8 +100,13 @@
         low_ref[at] = low
         both = ((0,), (0,))
         total = product(k_ref[:, span], high, both) + product(k_ref[:, span], low, both)
-        sums[at] = total
-        sums_out[at] = total.astype(jnp.bfloat16)
+        sums[0, at] = total[:, :hd]
+        sums[1, at] = total[:, hd:]
+        sums_out[at] = sums[far, at].astype(jnp.bfloat16)
+        if at == 0:
+            pl.semaphore_wait(
+                barrier, pairs + 1 + not_first.astype(jnp.int32) + not_last.astype(jnp.int32)
+            )
         send = pltpu.make_async_remote_copy(
             sums_out.at[at], sums_in.at[at], ss_sem.at[at], sr_sem.at[at],
             device_id={"seq": twin_seq}, device_id_type=MESH,
@@ -134,33 +136,72 @@
         qn_ref[at] = q
         first[at] = within(at, split(q))
 
+    bits = run_out.shape[1]
+    bit = hd // bits
+    run_sends = [
+        [
+            pltpu.make_async_remote_copy(
+                run_out.at[at, piece], run_in.at[at, piece],
+                rs_sem.at[at, piece], rr_sem.at[at, piece],
+                device_id={"seq": (seq + 2) % seqs}, device_id_type=MESH,
+            )
+            for piece in range(bits)
+        ]
+        for at in range(heads)
+    ]
+    past_sends = [
+        [
+            pltpu.make_async_remote_copy(
+                past_out.at[at, piece], past_in.at[at, piece],
+                as_sem.at[at, piece], ar_sem.at[at, piece],
+                device_id={"seq": twin_seq}, device_id_type=MESH,
+            )
+            for piece in range(bits)
+        ]
+        for at in range(heads)
+    ]
+
+    @pl.when(rank == 0)
+    def _():
+        run_in[...] = jnp.zeros(run_in.shape, run_in.dtype)
+
+    def advance(at):
+        sum_sends[at].wait_recv()
+        for piece in range(bits):
+            span = slice(piece * bit, (piece + 1) * bit)
+
+            @pl.when(not_first)
+            def _():
+                run_sends[at][piece].wait_recv()
+
+            @pl.when(not_last)
+            def _():
+                run_out[at, piece] = run_in[at, piece] + (
+                    sums[near, at, span] + sums_in[at, span].astype(jnp.float32)
+                )
+                run_sends[at][piece].start()
+
+            mine = jnp.where(side == 0, sums[near, at, span], 0.0)
+            past_out[at, piece] = (run_in[at, piece] + mine).astype(jnp.bfloat16)
+            past_sends[at][piece].start()
+
     mixed_sends = []
-    run_sends = []
-    for at in range(heads):
-        run_sends.append(pltpu.make_async_remote_copy(
-            run_out.at[at], run_in.at[at], rs_sem.at[at], rr_sem.at[at],
-            device_id={"seq": (seq + 2) % seqs}, device_id_type=MESH,
-        ))
-
-        @pl.when(rank == 0)
-        def _():
-            run_in[at] = jnp.zeros(run_in.shape[1:], run_in.dtype)
-
-        sum_sends[at].wait_recv()
-
-        @pl.when(not_first)
-        def _():
-            run_sends[at].wait_recv()
-
-        @pl.when(not_last)
-        def _():
-            run_out[at] = (
-                run_in[at].astype(jnp.float32) + (sums[at] + sums_in[at].astype(jnp.float32))
-            ).astype(jnp.bfloat16)
-            run_sends[at].start()
-
-        near = jnp.where(side == 1, sums_in[at], jnp.zeros(sums_in.shape[1:], jnp.bfloat16))
-        state = jnp.concatenate([run_in[at], near], axis=0)
+
+    def solve(at):
+        before = jnp.where(side == 1, sums_in[at].astype(jnp.float32), 0.0)
+        held, rest = split(run_in[at].reshape(hd, hd) + before)
+        for piece in range(bits):
+            past_sends[at][piece].wait_recv()
+        given = past_in[at].reshape(hd, hd)
+        none = jnp.zeros((hd, hd), jnp.bfloat16)
+        left = side == 0
+        state = jnp.concatenate(
+            [
+                jnp.concatenate([jnp.where(left, held, given), jnp.where(left, given, held)], axis=1),
+                jnp.concatenate([jnp.where(left, rest, none), jnp.where(left, none, rest)], axis=1),
+            ],
+            axis=0,
+        )
 
         def carried(parts):
             high, low = parts
@@ -190,46 +231,59 @@
         send.start()
         mixed_sends.append(send)
 
+    advance(0)
+    for at in range(1, heads):
+        advance(at)
+        solve(at - 1)
+    solve(heads - 1)
+
     for load in w_loads:
         load.wait()
     for send in w_sends:
         send.wait_recv()
-    for send in mixed_sends:
+    for send in mixed_sends[:-1]:
         send.wait_recv()
-
-    def projected(index, rows):
-        return product(mixed[rows, :], w_own[index]) + product(mixed_in[rows, :], w_other[index])
+    most = (heads - 1) * hd
+
+    def begun(index, rows):
+        return product(mixed[rows, :], w_own[index]) + product(
+            mixed_in[rows, :most], w_other[index, :most, :]
+        )
+
+    def ended(index, rows):
+        return product(mixed_in[rows, most:], w_other[index, most:, :])
 
     cuts = part_out.shape[1]
     cut = tokens // cuts
     part_sends = []
-    for off in range(1, pairs):
-        target = (pair + off) % pairs
-        for piece in range(cuts):
-            part_out[off - 1, piece] = projected(
-                target, slice(piece * cut, (piece + 1) * cut)
-            ).astype(jnp.bfloat16)
+    pieces = [slice(piece * cut, (piece + 1) * cut) for piece in range(cuts)]
+    order = [(pair + off) % pairs for off in range(1, pairs)]
+    starts = [[begun(target, rows) for rows in pieces] for target in order]
+    mixed_sends[-1].wait_recv()
+    for off, target in enumerate(order):
+        for piece, rows in enumerate(pieces):
+            part_out[off, piece] = (starts[off][piece] + ended(target, rows)).astype(jnp.bfloat16)
             send = pltpu.make_async_remote_copy(
-                part_out.at[off - 1, piece], part_in.at[off - 1, piece],
-                ps_sem.at[off - 1, piece], pr_sem.at[off - 1, piece],
+                part_out.at[off, piece], part_in.at[off, piece],
+                ps_sem.at[off, piece], pr_sem.at[off, piece],
                 device_id={"head": 2 * target + lane}, device_id_type=MESH,
             )
             send.start()
             part_sends.append(send)
-    own = [projected(pair, slice(piece * cut, (piece + 1) * cut)) for piece in range(cuts)]
-    for piece in range(cuts):
+    own = [begun(pair, rows) + ended(pair, rows) for rows in pieces]
+    for piece, rows in enumerate(pieces):
         total = own[piece]
-        for off in range(1, pairs):
-            part_sends[(off - 1) * cuts + piece].wait_recv()
-            total = total + part_in[off - 1, piece].astype(jnp.float32)
-        out_ref[piece * cut:(piece + 1) * cut, :] = total.astype(out_ref.dtype)
-
-    for send in sum_sends + w_sends + mixed_sends + part_sends:
+        for off in range(pairs - 1):
+            part_sends[off * cuts + piece].wait_recv()
+            total = total + part_in[off, piece].astype(jnp.float32)
+        out_ref[rows, :] = total.astype(out_ref.dtype)
+
+    for send in sum_sends + w_sends + mixed_sends + part_sends + sum(past_sends, []):
         send.wait_send()
 
     @pl.when(not_last)
     def _():
-        for send in run_sends:
+        for send in sum(run_sends, []):
             send.wait_send()
 
 
@@ -243,7 +297,7 @@
         rows, model = out_weight.shape
         width = model // groups
         pairs = groups // 2
-        cuts = 4
+        cuts, bits = 4, 2
         bf16, f32 = jnp.bfloat16, jnp.float32
         dma = pltpu.SemaphoreType.DMA
         others = max(pairs - 1, 1)
@@ -261,11 +315,13 @@
                 pltpu.VMEM((pairs, rows, width), bf16),
                 pltpu.VMEM((heads, tokens, 2 * hd), bf16),
                 pltpu.VMEM((heads, tokens, 2 * hd), bf16),
-                pltpu.VMEM((heads, hd, 2 * hd), f32),
-                pltpu.VMEM((heads, hd, 2 * hd), bf16),
-                pltpu.VMEM((heads, hd, 2 * hd), bf16),
-                pltpu.VMEM((heads, hd, 2 * hd), bf16),
-                pltpu.VMEM((heads, hd, 2 * hd), bf16),
+                pltpu.VMEM((2, heads, hd, hd), f32),
+                pltpu.VMEM((heads, hd, hd), bf16),
+                pltpu.VMEM((heads, hd, hd), bf16),
+                pltpu.VMEM((heads, bits, hd // bits, hd), f32),
+                pltpu.VMEM((heads, bits, hd // bits, hd), f32),
+                pltpu.VMEM((heads, bits, hd // bits, hd), bf16),
+                pltpu.VMEM((heads, bits, hd // bits, hd), bf16),
                 pltpu.VMEM((heads, tokens, hd), f32),
                 pltpu.VMEM((heads, tokens, 2 * hd), f32),
                 pltpu.VMEM((tokens, wide), bf16),
@@ -273,11 +329,12 @@
                 pltpu.VMEM((others, cuts, tokens // cuts, width), bf16),
                 pltpu.VMEM((others, cuts, tokens // cuts, width), bf16),
                 dma((3,)), dma((pairs,)), dma((pairs,)), dma((pairs,)),
-                dma((heads,)), dma((heads,)), dma((heads,)), dma((heads,)),
+                dma((heads,)), dma((heads,)),
+                dma((heads, bits)), dma((heads, bits)), dma((heads, bits)), dma((heads, bits)),
                 dma((heads,)), dma((heads,)), dma((others, cuts)), dma((others, cuts)),
             ],
             compiler_params=pltpu.CompilerParams(
-                collective_id=0, has_side_effects=True, vmem_limit_bytes=48 * 2**20
+                collective_id=0, has_side_effects=True, vmem_limit_bytes=63 * 2**20
             ),
         )(queries, keys, values, ridges, out_weight)
 

time: 36.7 us -> 35.7 us (0.973)
  local copies, waits for them, and re-layouts: 5.8 us -> 1.67 us
  Pallas kernels: 30.6 us -> 33.9 us
    unnamed x11 -> x1, local copies, waits for them, and re-layouts: 5.8 us -> 1.67 us
    pallas_call x1, Pallas kernels: 30.6 us -> 33.9 us  [shards(): pl.pallas_call(functools.partial(kernel, seqs, groups, heads), out_shape=...]
where the time goes in v2:
time: 35.7 us; the launch traced here: 35.5 us
  Pallas kernels  33.9 us (95%)
  local copies, waits for them, and re-layouts  1.67 us (5%)
    pallas_call x1, Pallas kernels, shards(): pl.pallas_call(functools.partial(kernel, seqs, groups, heads), out_shape=...  33.9 us
    unnamed x1, local copies, waits for them, and re-layouts  1.67 us

profile of v2, /device:TPU:25, one launch (start us, length us, event | category | flops | bytes accessed | tf_op | source)
XLA Modules:
  0.0 35.5 jit_solution(10813711424903633867)
XLA Ops:
  0.0 33.9 %shard_map.55 = bf16[256,512]{1,0:T(8,128)(2,1)} custom-call(bf16[256,512]{1,0:T(8,128)(2,1)} %q_any.1, bf16[256,512]{1,0:T(8,128)(2,1)} %k_any.1, bf16[256,512]{1,0:T(8,128)(2,1)} %v_any.1, f32[4]{0:T(128)} %ridge_ref.1, bf16[512,2048]{1,0:T(8,128)(2,1)} %w_any.1), custom_call_target="tpu_custom_call" | custom-call | tf_op jit(solution)/shard_map/pallas_call | solution.py:305
  33.9 1.7 %copy.7 = bf16[256,512]{1,0:T(8,128)(2,1)} copy(bf16[256,512]{1,0:T(8,128)(2,1)} %shard_map.55) | data formatting | bytes 524288
